TPU v7x, 256 devices: a whole 4x4x8 slice. The times are simulated.
256 devices in a mesh: dp: 32 (over y, z), head: 4 (over x), rep: 2 (over core).
Axes of the slice: x: 4, y: 4, z: 8, core: 2. Of those that a mesh axis runs over, the one named last changes fastest.
Arguments:
- embeddings: bfloat16 [16384, 8, 1152], P(('dp', 'head', 'rep')), may hold values from -6 to 6
- coverage: int32 [16384, 2], P(('dp', 'head', 'rep')), may hold values from 0 to 127, all different within a row; in each aligned block of 64 rows (0 to 63, 64 to 127, ...) at most 2 rows name the same one
- labels: int32 [16384, 2, 8], P(('dp', 'head', 'rep')), may hold values 0 or 1
- w_in: bfloat16 [128, 1152, 768], P(('dp', 'head')), may hold values from -0.1875 to 0.1875
- bias_in: bfloat16 [128, 768], P(('dp', 'head')), may hold values from -3 to 3
- w_out: bfloat16 [128, 768], P(('dp', 'head')), may hold values from -0.21875 to 0.21875
- first_w: float32 [128, 1152, 768], P(('dp', 'head'), 'rep'), may hold values from -0.5 to 0.5
- second_w: float32 [128, 1152, 768], P(('dp', 'head'), 'rep'), may hold values from 0.0001 to 0.001
- first_vec: float32 [128, 2, 768], P(('dp', 'head')), may hold values from -0.5 to 0.5
- second_vec: float32 [128, 2, 768], P(('dp', 'head')), may hold values from 0.0001 to 0.01
Outputs:
- new_w_in: bfloat16 [128, 1152, 768], P(('dp', 'head'))
- new_vec: bfloat16 [128, 2, 768], P(('dp', 'head'))
- new_first_w: float32 [128, 1152, 768], P(('dp', 'head'), 'rep')
- new_second_w: float32 [128, 1152, 768], P(('dp', 'head'), 'rep')
- new_first_vec: float32 [128, 2, 768], P(('dp', 'head'))
- new_second_vec: float32 [128, 2, 768], P(('dp', 'head'))
Inputs may be any that keep to these rules, and one draw needn't show every extreme that they name: `coverage`: each block names 2 different heads. Among the 64 blocks of one device (aligned blocks of rows, in order) no head is named more than 2 times, a bound that some block reaches; every head is named by some block.
All inputs are finite; a program needn't handle non-finite values. No bound on the sum of `labels` on one device may be relied on, other than what follows from the above.
Results may differ from a plain program's by a relative error of at most 0.00155.
Values may be sent and summed in bfloat16 or wider, within the bound.
A program may use at most 128 MiB of HBM per device.

v0:
```python
import jax
import jax.numpy as jnp
from jax import lax
from jax.sharding import PartitionSpec as P

beta_one = 0.9
beta_two = 0.999
learn_rate = 0.001
epsilon = 1e-08


def per_device(
    embeddings, coverage, labels, w_in, bias_in, w_out, first_w, second_w, first_vec, second_vec
):
    dp_count = lax.axis_size("dp")
    head_count = lax.axis_size("head")
    owners = dp_count * head_count
    block_count, rows_block, feature = embeddings.shape
    per_block = coverage.shape[1]
    slot_count = 2 * block_count * per_block // owners
    entries = block_count * per_block
    heads_flat = coverage.reshape(entries)
    onehot = (heads_flat[:, None] == jnp.arange(owners, dtype=jnp.int32)[None, :]).astype(jnp.int32)
    slot_rank = jnp.sum((jnp.cumsum(onehot, axis=0) - 1) * onehot, axis=1)
    target_slot = heads_flat * slot_count + slot_rank
    picker = jnp.arange(owners * slot_count, dtype=jnp.int32)[:, None] == target_slot[None, :]
    block_pick = jnp.sum(
        picker.reshape(owners * slot_count, block_count, per_block).astype(jnp.int32), axis=2
    ).astype(jnp.bfloat16)
    send_rows = jnp.dot(
        block_pick,
        embeddings.reshape(block_count, rows_block * feature),
        preferred_element_type=jnp.float32,
    ).astype(jnp.bfloat16)
    label_marks = (labels.reshape(entries, rows_block) + 1).astype(jnp.float32)
    send_marks = jnp.dot(
        picker.astype(jnp.float32), label_marks, precision=lax.Precision.HIGHEST
    ).astype(jnp.bfloat16)
    direct_rows = send_rows.reshape(owners, slot_count, rows_block, feature)
    direct_marks = send_marks.reshape(owners, slot_count, rows_block)
    got_rows, got_marks = (
        lax.all_to_all(direct_rows, ("dp", "head"), split_axis=0, concat_axis=0, tiled=True),
        lax.all_to_all(direct_marks, ("dp", "head"), split_axis=0, concat_axis=0, tiled=True),
    )
    row_data = got_rows.reshape(-1, feature)
    marks_all = got_marks.reshape(-1).astype(jnp.float32)
    usable = marks_all > 0.5
    target = marks_all - 1.0
    out_weight = w_out[0].astype(jnp.float32)
    pre_act = (
        jnp.dot(row_data, w_in[0], preferred_element_type=jnp.float32)
        + bias_in[0].astype(jnp.float32)[None, :]
    )
    sig_pre = jax.nn.sigmoid(pre_act)
    hidden = pre_act * sig_pre
    logits = jnp.sum(hidden * out_weight[None, :], axis=1)
    residual = jnp.where(usable, jax.nn.sigmoid(logits) - target, jnp.zeros_like(logits))
    grad_pre = residual[:, None] * out_weight[None, :] * sig_pre * (1.0 + pre_act * (1.0 - sig_pre))
    grad_low = grad_pre.astype(jnp.bfloat16)
    vec_part = jnp.stack([jnp.sum(grad_pre, axis=0), jnp.sum(residual[:, None] * hidden, axis=0)])
    half_rows = feature // lax.axis_size("rep")
    first_row = lax.axis_index("rep") * half_rows
    full_part = lax.dot_general(
        row_data, grad_low, (((0,), (0,)), ((), ())), preferred_element_type=jnp.float32
    )
    whole_w, grad_vec = lax.psum((full_part, vec_part), "rep")
    grad_w = lax.dynamic_slice_in_dim(whole_w, first_row, half_rows, 0)
    new_first_w = beta_one * first_w[0] + (1.0 - beta_one) * grad_w
    new_second_w = beta_two * second_w[0] + (1.0 - beta_two) * grad_w * grad_w
    old_rows = lax.dynamic_slice_in_dim(w_in[0], first_row, half_rows, 0).astype(jnp.float32)
    new_half = (old_rows - learn_rate * new_first_w / (jnp.sqrt(new_second_w) + epsilon)).astype(
        jnp.bfloat16
    )
    new_w_in = lax.all_gather(new_half, "rep", axis=0, tiled=True)
    vector = jnp.stack([bias_in[0], w_out[0]]).astype(jnp.float32)
    new_first_vec = beta_one * first_vec[0] + (1.0 - beta_one) * grad_vec
    new_second_vec = beta_two * second_vec[0] + (1.0 - beta_two) * grad_vec * grad_vec
    new_vec = (vector - learn_rate * new_first_vec / (jnp.sqrt(new_second_vec) + epsilon)).astype(
        jnp.bfloat16
    )
    return (
        new_w_in[None],
        new_vec[None],
        new_first_w[None],
        new_second_w[None],
        new_first_vec[None],
        new_second_vec[None],
    )


def solution(mesh):
    placed = (
        P(("dp", "head", "rep"), None, None),
        P(("dp", "head", "rep"), None),
        P(("dp", "head", "rep"), None, None),
        P(("dp", "head"), None, None),
        P(("dp", "head"), None),
        P(("dp", "head"), None),
        P(("dp", "head"), "rep", None),
        P(("dp", "head"), "rep", None),
        P(("dp", "head"), None, None),
        P(("dp", "head"), None, None),
    )
    return jax.shard_map(
        per_device,
        mesh=mesh,
        in_specs=placed,
        out_specs=(
            P(("dp", "head"), None, None),
            P(("dp", "head"), None, None),
            P(("dp", "head"), "rep", None),
            P(("dp", "head"), "rep", None),
            P(("dp", "head"), None, None),
            P(("dp", "head"), None, None),
        ),
        check_vma=False,
    )
```

profile of v0, /device:TPU:1, one launch (start us, length us, event | category | flops | bytes accessed | tf_op | source)
XLA Modules:
  0.0 236.4 jit_solution(17417560200644279252)
XLA Ops:
  7.2 0.8 copy.30
  8.5 0.7 add_convert_fusion
  9.3 0.2 convolution_convert_fusion.1
  9.5 0.8 copy.33
  10.3 16.3 %all-to-all-start.1 = ((bf16[128,2,8]{2,1,0:T(2,128)(2,1)}), bf16[128,2,8]{2,1,0:T(2,128)(2,1)S(1)}, u32[]{:S(2)}, u32[]{:S(2)}) async-start(bf16[128,2,8]{2,1,0:T(2,128)(2,1)} %bitcast.4), calls=%async_computation.1 | async-start | bytes 131072 | tf_op jit(solution)/shard_map/all_to_all | solution.py:43
  26.8 1.5 copy.34
  28.3 0.7 multiply_add_fusion
  29.1 1.4 convolution_convert_fusion
  30.5 3.1 %copy.35 = bf16[32,8,8,1152]{3,2,1,0:T(8,128)(2,1)} copy(bf16[32,8,8,1152]{3,1,2,0:T(8,128)(2,1)S(1)} %bitcast.56) | data formatting | bytes 9437184
  33.6 3.6 %all-to-all-done.1 = bf16[128,2,8]{2,1,0:T(2,128)(2,1)S(1)} async-done(((bf16[128,2,8]{2,1,0:T(2,128)(2,1)}), bf16[128,2,8]{2,1,0:T(2,128)(2,1)S(1)}, u32[]{:S(2)}, u32[]{:S(2)}) %all-to-all-start.1) | async-done | bytes 4128 | tf_op jit(solution)/shard_map/all_to_all | solution.py:43
  37.2 10.3 %all-to-all-start = ((bf16[128,2,8,1152]{3,2,1,0:T(8,128)(2,1)}), bf16[128,2,8,1152]{3,2,1,0:T(8,128)(2,1)}, u32[]{:S(2)}, u32[]{:S(2)}) async-start(bf16[128,2,8,1152]{3,2,1,0:T(8,128)(2,1)} %bitcast.55), calls=%async_computation | async-start | bytes 9437184 | tf_op jit(solution)/shard_map/all_to_all | solution.py:42
  47.5 0.2 all-reduce.2.cloned.1.call-start
  48.0 0.2 sub.27
  48.2 103.3 %all-to-all-done = bf16[128,2,8,1152]{3,2,1,0:T(8,128)(2,1)} async-done(((bf16[128,2,8,1152]{3,2,1,0:T(8,128)(2,1)}), bf16[128,2,8,1152]{3,2,1,0:T(8,128)(2,1)}, u32[]{:S(2)}, u32[]{:S(2)}) %all-to-all-start) | async-done | bytes 4718624 | tf_op jit(solution)/shard_map/all_to_all | solution.py:42
  151.5 7.0 %multiply_reduce_fusion.1 = (f32[2048]{0:T(1024)S(1)}, f32[2048,768]{1,0:T(8,128)S(1)}) fusion(f32[768]{0:T(1024)S(1)} %get-tuple-element.16, f32[768]{0:T(1024)S(1)} %get-tuple-element.17, bf16[2048,1152]{1,0:T(8,128)(2,1)} %bitcast.2, bf16[1,1152,768]{2,1,0:T(8,128)(2,1)S(1)} %copy-done.3), kind=kOutput, calls=%fused_computation.3 | convolution fusion | flops 3634886656 | bytes 12793856 | tf_op jit(solution)/shard_map/dot_general | solution.py:51
  158.6 2.6 %copy-done = f32[2048,768]{1,0:T(8,128)} copy-done((f32[2048,768]{1,0:T(8,128)}, f32[2048,768]{1,0:T(8,128)S(1)}, u32[]{:S(2)}) %copy-start) | copy-done | bytes 6291480
  161.2 9.1 %fusion.1 = f32[1152,768]{1,0:T(8,128)} fusion(bf16[2048,1152]{1,0:T(8,128)(2,1)} %bitcast.2, f32[2048,768]{1,0:T(8,128)S(1)} %get-tuple-element.15, f32[2048]{0:T(1024)S(1)} %subtract_select_fusion, f32[768]{0:T(1024)S(1)} %get-tuple-element.16, f32[768]{0:T(1024)S(1)} %get-tuple-element.17), kind=kOutput, calls=%fused_computation.6 | convolution fusion | flops 3641180160 | bytes 14563328 | tf_op jit(solution)/shard_map/dot_general | solution.py:63
  170.4 34.5 %all-reduce.2.cloned.1.call-done = f32[1152,768]{1,0:T(8,128)} async-done(((f32[1152,768]{1,0:T(8,128)}), f32[1152,768]{1,0:T(8,128)}) %all-reduce.2.cloned.1.call-update) | async-done | bytes 3538960 | tf_op jit(solution)/shard_map/psum | solution.py:66
  204.9 4.9 %fusion.8 = (f32[1,576,768]{2,1,0:T(8,128)}, bf16[576,768]{1,0:T(8,128)(2,1)}, f32[1,576,768]{2,1,0:T(8,128)}) fusion(f32[1152,768]{1,0:T(8,128)} %all-reduce.2.cloned.1.call-done, s32[]{:T(128)S(6)} %select_n.12, f32[1,576,768]{2,1,0:T(8,128)S(1)} %copy-done.1, f32[1,576,768]{2,1,0:T(8,128)S(1)} %copy-done.2, bf16[1,1152,768]{2,1,0:T(8,128)(2,1)} %param.13), kind=kLoop, calls=%fused_computation.17 | loop fusion | flops 5750784 | bytes 10616836 | tf_op jit(solution)/shard_map/broadcast_in_dim | solution.py:85
  209.9 5.3 %fusion.16 = (f32[768]{0:T(1024)S(1)}, f32[768]{0:T(1024)S(1)}) fusion(f32[2048,768]{1,0:T(8,128)} %copy-done, f32[768]{0:T(1024)S(1)} %get-tuple-element.17, f32[768]{0:T(1024)S(1)} %get-tuple-element.16, f32[2048]{0:T(1024)S(1)} %subtract_select_fusion), kind=kLoop, calls=%fused_computation.42 | loop fusion | flops 22018560 | bytes 6311936 | tf_op jit(solution)/shard_map/reduce_sum | solution.py:60
  215.2 2.5 %psum.15 = f32[2,768]{1,0:T(2,128)S(1)} all-reduce(f32[2,768]{1,0:T(2,128)S(1)} %pad_maximum_fusion), channel_id=1, replica_groups=mesh['dp'=32,'head'=4,'rep'=2] {'rep'}, use_global_device_ids=true, to_apply=%region_7.8 | all-reduce | flops 1536 | bytes 12288 | tf_op jit(solution)/shard_map/psum | solution.py:66
  217.7 0.6 fusion.15
  218.4 8.4 %all-gather.2.cloned.1.call-done = bf16[1152,768]{1,0:T(8,128)(2,1)} async-done(((bf16[576,768]{1,0:T(8,128)(2,1)}), bf16[1152,768]{1,0:T(8,128)(2,1)}) %all-gather.2.cloned.1.call-update) | async-done | bytes 1769488 | tf_op jit(solution)/shard_map/all_gather | solution.py:74
  226.8 2.8 %copy.38 = bf16[1,1152,768]{2,1,0:T(8,128)(2,1)} copy(bf16[1,1152,768]{2,1,0:T(8,128)(2,1)} %bitcast.58) | data formatting | bytes 3538944
  (39 shorter events, 1.4 us)
Async XLA Ops:
  10.3 26.9 %all-to-all-start.1 = ((bf16[128,2,8]{2,1,0:T(2,128)(2,1)}), bf16[128,2,8]{2,1,0:T(2,128)(2,1)S(1)}, u32[]{:S(2)}, u32[]{:S(2)}) async-start(bf16[128,2,8]{2,1,0:T(2,128)(2,1)} %bitcast.4), calls=%async_computation.1 | async-start | bytes 131072 | tf_op jit(solution)/shard_map/all_to_all | solution.py:43
  37.2 10.5 %copy-start.4 = (bf16[1,768]{1,0:T(2,128)(2,1)S(1)}, bf16[1,768]{1,0:T(2,128)(2,1)}, u32[]{:S(2)}) copy-start(bf16[1,768]{1,0:T(2,128)(2,1)} %param.15) | copy-start | bytes 4612
  37.2 10.5 %copy-start.6 = (bf16[1,768]{1,0:T(2,128)(2,1)S(1)}, bf16[1,768]{1,0:T(2,128)(2,1)}, u32[]{:S(2)}) copy-start(bf16[1,768]{1,0:T(2,128)(2,1)} %param.14) | copy-start | bytes 4612
  37.2 114.4 %copy-start.3 = (bf16[1,1152,768]{2,1,0:T(8,128)(2,1)S(1)}, bf16[1,1152,768]{2,1,0:T(8,128)(2,1)}, u32[]{:S(2)}) copy-start(bf16[1,1152,768]{2,1,0:T(8,128)(2,1)} %param.13) | copy-start | bytes 5308420
  37.2 114.4 %all-to-all-start = ((bf16[128,2,8,1152]{3,2,1,0:T(8,128)(2,1)}), bf16[128,2,8,1152]{3,2,1,0:T(8,128)(2,1)}, u32[]{:S(2)}, u32[]{:S(2)}) async-start(bf16[128,2,8,1152]{3,2,1,0:T(8,128)(2,1)} %bitcast.55), calls=%async_computation | async-start | bytes 9437184 | tf_op jit(solution)/shard_map/all_to_all | solution.py:42
  47.5 157.4 %all-reduce.2.cloned.1.call-start = ((), (), s32[]{:S(2)}) async-start(), calls=%async_computation.2 | async-start | bytes 7077888 | tf_op jit(solution)/shard_map/psum | solution.py:66
  158.5 2.7 %copy-start = (f32[2048,768]{1,0:T(8,128)}, f32[2048,768]{1,0:T(8,128)S(1)}, u32[]{:S(2)}) copy-start(f32[2048,768]{1,0:T(8,128)S(1)} %get-tuple-element.15) | copy-start | bytes 18874372
  170.3 34.6 %copy-start.1 = (f32[1,576,768]{2,1,0:T(8,128)S(1)}, f32[1,576,768]{2,1,0:T(8,128)}, u32[]{:S(2)}) copy-start(f32[1,576,768]{2,1,0:T(8,128)} %param.17) | copy-start | bytes 5308420
  170.3 34.6 %copy-start.2 = (f32[1,576,768]{2,1,0:T(8,128)S(1)}, f32[1,576,768]{2,1,0:T(8,128)}, u32[]{:S(2)}) copy-start(f32[1,576,768]{2,1,0:T(8,128)} %param.16) | copy-start | bytes 5308420
  170.3 56.5 %all-gather.2.cloned.1.call-start = ((), (), s32[]{:S(2)}) async-start(), calls=%async_computation.3 | async-start | bytes 2654208 | tf_op jit(solution)/shard_map/all_gather | solution.py:74
  209.9 7.9 %copy-start.5 = (bf16[1,768]{1,0:T(2,128)(2,1)S(1)}, bf16[1,768]{1,0:T(2,128)(2,1)}, u32[]{:S(2)}) copy-start(bf16[1,768]{1,0:T(2,128)(2,1)} %param.15) | copy-start | bytes 4612
  209.9 7.9 %copy-start.7 = (bf16[1,768]{1,0:T(2,128)(2,1)S(1)}, bf16[1,768]{1,0:T(2,128)(2,1)}, u32[]{:S(2)}) copy-start(bf16[1,768]{1,0:T(2,128)(2,1)} %param.14) | copy-start | bytes 4612
  209.9 7.9 %copy-start.8 = (f32[1,2,768]{2,1,0:T(2,128)S(1)}, f32[1,2,768]{2,1,0:T(2,128)}, u32[]{:S(2)}) copy-start(f32[1,2,768]{2,1,0:T(2,128)} %param.19) | copy-start | bytes 18436
  209.9 7.9 %copy-start.9 = (f32[1,2,768]{2,1,0:T(2,128)S(1)}, f32[1,2,768]{2,1,0:T(2,128)}, u32[]{:S(2)}) copy-start(f32[1,2,768]{2,1,0:T(2,128)} %param.18) | copy-start | bytes 18436
Sparse Core Ops, SparseCore 0:
  170.4 34.4 all-reduce.1
  210.0 16.7 all-gather.1
where the time goes:
time: 237 us; the launch traced here: 236 us
  waiting for transfers between devices  150 us (63%)
  starting transfers between devices  26.9 us (11%)
  matrix products  17.7 us (7%)
  between operations  14.3 us (6%)
  other arithmetic  13 us (5%)
  local copies, waits for them, and re-layouts  12.3 us (5%)
  blocking collectives  2.51 us (1%)
    all_to_all x1, waiting for transfers between devices, per_device(): lax.all_to_all(direct_rows, ('dp', 'head'), split_axis=0, concat_axis=0,...  103 us
    psum x1, waiting for transfers between devices, per_device(): whole_w, grad_vec = lax.psum((full_part, vec_part), 'rep')  34.5 us
    all_to_all x1, starting transfers between devices, per_device(): lax.all_to_all(direct_marks, ('dp', 'head'), split_axis=0, concat_axis=0,...  16.3 us
    unnamed x24, local copies, waits for them, and re-layouts  10.8 us
    all_to_all x1, starting transfers between devices, per_device(): lax.all_to_all(direct_rows, ('dp', 'head'), split_axis=0, concat_axis=0,...  10.3 us
    dot_general x1, matrix products, per_device(): lax.dot_general(row_data, grad_low, (((0,), (0,)), ((), ())), preferred_e...  9.07 us
    all_gather x1, waiting for transfers between devices, per_device(): new_w_in = lax.all_gather(new_half, 'rep', axis=0, tiled=True)  8.39 us
    dot_general x1, matrix products, per_device(): jnp.dot(row_data, w_in[0], preferred_element_type=jnp.float32)  7 us
  transfers between devices with their start and end apart: 4, of which 4 were waited for; matrix products, arithmetic and copies ran while one was open for 6% of the time, Pallas kernels for 0%

commit v1 on v0

--- a/solution.py
+++ b/solution.py
@@ -71,7 +71,9 @@
     new_half = (old_rows - learn_rate * new_first_w / (jnp.sqrt(new_second_w) + epsilon)).astype(
         jnp.bfloat16
     )
-    new_w_in = lax.all_gather(new_half, "rep", axis=0, tiled=True)
+    new_w_in = jnp.concatenate(
+        lax.all_to_all(jnp.stack(lax.axis_size("rep") * [new_half], axis=0), "rep", 0, 0), axis=0
+    )
     vector = jnp.stack([bias_in[0], w_out[0]]).astype(jnp.float32)
     new_first_vec = beta_one * first_vec[0] + (1.0 - beta_one) * grad_vec
     new_second_vec = beta_two * second_vec[0] + (1.0 - beta_two) * grad_vec * grad_vec

time: 237 us -> 223 us (0.941)
  waiting for transfers between devices: 150 us -> 128 us
  blocking collectives: 2.51 us -> 11.7 us
    psum x1, waiting for transfers between devices: 34.5 us -> 21 us  [per_device(): whole_w, grad_vec = lax.psum((full_part, vec_part), 'rep')]
    all_gather x1 -> x0, waiting for transfers between devices: 8.39 us -> none  [per_device(): new_w_in = lax.all_gather(new_half, 'rep', axis=0, tiled=True)]
    all_to_all x0 -> x1, blocking collectives: none -> 5.01 us  [per_device(): lax.all_to_all(jnp.stack(lax.axis_size('rep') * [new_half], axis=0), 'rep...]
    psum x1, blocking collectives: 2.51 us -> 6.74 us  [per_device(): whole_w, grad_vec = lax.psum((full_part, vec_part), 'rep')]
    unnamed x24 -> x16, local copies, waits for them, and re-layouts: 10.8 us -> 9.15 us
  transfers between devices with their start and end apart: 4 -> 3, of which waited for: 4 -> 3; matrix products, arithmetic and copies ran while one was open for 6% -> 6% of each run, Pallas kernels for 0% -> 0%
where the time goes in v1:
time: 223 us
  waiting for transfers between devices  128 us (57%)
  starting transfers between devices  26.8 us (12%)
  matrix products  17.7 us (8%)
  between operations  14.2 us (6%)
  other arithmetic  13.7 us (6%)
  blocking collectives  11.7 us (5%)
  local copies, waits for them, and re-layouts  10.7 us (5%)
    all_to_all x1, waiting for transfers between devices, per_device(): lax.all_to_all(direct_rows, ('dp', 'head'), split_axis=0, concat_axis=0,...  103 us
    psum x1, waiting for transfers between devices, per_device(): whole_w, grad_vec = lax.psum((full_part, vec_part), 'rep')  21 us
    all_to_all x1, starting transfers between devices, per_device(): lax.all_to_all(direct_marks, ('dp', 'head'), split_axis=0, concat_axis=0,...  16.3 us
    all_to_all x1, starting transfers between devices, per_device(): lax.all_to_all(direct_rows, ('dp', 'head'), split_axis=0, concat_axis=0,...  10.3 us
    unnamed x16, local copies, waits for them, and re-layouts  9.15 us
    dot_general x1, matrix products, per_device(): lax.dot_general(row_data, grad_low, (((0,), (0,)), ((), ())), preferred_e...  9.07 us
    dot_general x1, matrix products, per_device(): jnp.dot(row_data, w_in[0], preferred_element_type=jnp.float32)  7 us
    psum x1, blocking collectives, per_device(): whole_w, grad_vec = lax.psum((full_part, vec_part), 'rep')  6.74 us
  transfers between devices with their start and end apart: 3, of which 3 were waited for; matrix products, arithmetic and copies ran while one was open for 6% of the time, Pallas kernels for 0%

profile of v1, /device:TPU:1, one launch (start us, length us, event | category | flops | bytes accessed | tf_op | source)
XLA Modules:
  0.0 222.8 jit_solution(6301524641128057739)
XLA Ops:
  7.2 0.8 copy.30
  8.5 0.7 add_convert_fusion
  9.3 0.2 convolution_convert_fusion.1
  9.5 0.8 copy.33
  10.3 16.3 %all-to-all-start.1 = ((bf16[128,2,8]{2,1,0:T(2,128)(2,1)}), bf16[128,2,8]{2,1,0:T(2,128)(2,1)S(1)}, u32[]{:S(2)}, u32[]{:S(2)}) async-start(bf16[128,2,8]{2,1,0:T(2,128)(2,1)} %bitcast.4), calls=%async_computation.1 | async-start | bytes 131072 | tf_op jit(solution)/shard_map/all_to_all | solution.py:43
  26.8 1.5 copy.34
  28.3 0.7 multiply_add_fusion
  29.1 1.4 convolution_convert_fusion
  30.5 3.1 %copy.35 = bf16[32,8,8,1152]{3,2,1,0:T(8,128)(2,1)} copy(bf16[32,8,8,1152]{3,1,2,0:T(8,128)(2,1)S(1)} %bitcast.60) | data formatting | bytes 9437184
  33.6 3.6 %all-to-all-done.1 = bf16[128,2,8]{2,1,0:T(2,128)(2,1)S(1)} async-done(((bf16[128,2,8]{2,1,0:T(2,128)(2,1)}), bf16[128,2,8]{2,1,0:T(2,128)(2,1)S(1)}, u32[]{:S(2)}, u32[]{:S(2)}) %all-to-all-start.1) | async-done | bytes 4128 | tf_op jit(solution)/shard_map/all_to_all | solution.py:43
  37.2 10.3 %all-to-all-start = ((bf16[128,2,8,1152]{3,2,1,0:T(8,128)(2,1)}), bf16[128,2,8,1152]{3,2,1,0:T(8,128)(2,1)}, u32[]{:S(2)}, u32[]{:S(2)}) async-start(bf16[128,2,8,1152]{3,2,1,0:T(8,128)(2,1)} %bitcast.59), calls=%async_computation | async-start | bytes 9437184 | tf_op jit(solution)/shard_map/all_to_all | solution.py:42
  47.5 0.2 all-reduce.2.cloned.1.call-start
  48.0 0.2 sub.27
  48.2 103.3 %all-to-all-done = bf16[128,2,8,1152]{3,2,1,0:T(8,128)(2,1)} async-done(((bf16[128,2,8,1152]{3,2,1,0:T(8,128)(2,1)}), bf16[128,2,8,1152]{3,2,1,0:T(8,128)(2,1)}, u32[]{:S(2)}, u32[]{:S(2)}) %all-to-all-start) | async-done | bytes 4718624 | tf_op jit(solution)/shard_map/all_to_all | solution.py:42
  151.5 7.0 %multiply_reduce_fusion.1 = (f32[2048]{0:T(1024)S(1)}, f32[2048,768]{1,0:T(8,128)S(1)}) fusion(f32[768]{0:T(1024)S(1)} %get-tuple-element.16, f32[768]{0:T(1024)S(1)} %get-tuple-element.17, bf16[2048,1152]{1,0:T(8,128)(2,1)} %bitcast.2, bf16[1,1152,768]{2,1,0:T(8,128)(2,1)S(1)} %copy-done.3), kind=kOutput, calls=%fused_computation.3 | convolution fusion | flops 3634886656 | bytes 12793856 | tf_op jit(solution)/shard_map/dot_general | solution.py:51
  158.6 2.6 %copy-done = f32[2048,768]{1,0:T(8,128)} copy-done((f32[2048,768]{1,0:T(8,128)}, f32[2048,768]{1,0:T(8,128)S(1)}, u32[]{:S(2)}) %copy-start) | copy-done | bytes 6291480
  161.2 9.1 %fusion.1 = f32[1152,768]{1,0:T(8,128)} fusion(bf16[2048,1152]{1,0:T(8,128)(2,1)} %bitcast.2, f32[2048,768]{1,0:T(8,128)S(1)} %get-tuple-element.15, f32[2048]{0:T(1024)S(1)} %subtract_select_fusion, f32[768]{0:T(1024)S(1)} %get-tuple-element.16, f32[768]{0:T(1024)S(1)} %get-tuple-element.17), kind=kOutput, calls=%fused_computation.6 | convolution fusion | flops 3641180160 | bytes 14563328 | tf_op jit(solution)/shard_map/dot_general | solution.py:63
  170.3 5.4 %fusion.17 = (f32[768]{0:T(1024)S(1)}, f32[768]{0:T(1024)S(1)}) fusion(f32[2048,768]{1,0:T(8,128)} %copy-done, f32[768]{0:T(1024)S(1)} %get-tuple-element.17, f32[768]{0:T(1024)S(1)} %get-tuple-element.16, f32[2048]{0:T(1024)S(1)} %subtract_select_fusion), kind=kLoop, calls=%fused_computation.44 | loop fusion | flops 22018560 | bytes 6311936 | tf_op jit(solution)/shard_map/reduce_sum | solution.py:60
  175.8 6.7 %psum.15 = f32[2,768]{1,0:T(2,128)S(1)} all-reduce(f32[2,768]{1,0:T(2,128)S(1)} %pad_maximum_fusion.1), channel_id=1, replica_groups=mesh['dp'=32,'head'=4,'rep'=2] {'rep'}, use_global_device_ids=true, to_apply=%region_7.8 | all-reduce | flops 1536 | bytes 12288 | tf_op jit(solution)/shard_map/psum | solution.py:66
  182.5 1.4 fusion.16
  183.9 21.0 %all-reduce.2.cloned.1.call-done = f32[1152,768]{1,0:T(8,128)} async-done(((f32[1152,768]{1,0:T(8,128)}), f32[1152,768]{1,0:T(8,128)}) %all-reduce.2.cloned.1.call-update) | async-done | bytes 3538960 | tf_op jit(solution)/shard_map/psum | solution.py:66
  204.9 4.7 %fusion.9 = (f32[1,576,768]{2,1,0:T(8,128)}, bf16[1,576,768]{2,1,0:T(8,128)(2,1)S(1)}, f32[1,576,768]{2,1,0:T(8,128)}) fusion(f32[1152,768]{1,0:T(8,128)} %all-reduce.2.cloned.1.call-done, s32[]{:T(128)S(6)} %select_n.12, f32[1,576,768]{2,1,0:T(8,128)S(1)} %copy-done.1, f32[1,576,768]{2,1,0:T(8,128)S(1)} %copy-done.2, bf16[1,1152,768]{2,1,0:T(8,128)(2,1)} %param.13), kind=kLoop, calls=%fused_computation.19 | loop fusion | flops 5750784 | bytes 10616836 | tf_op jit(solution)/shard_map/broadcast_in_dim | solution.py:87
  209.7 5.0 %all_to_all.15 = bf16[2,576,768]{2,1,0:T(8,128)(2,1)S(1)} all-to-all(bf16[2,576,768]{2,1,0:T(8,128)(2,1)S(1)} %pad_maximum_fusion), channel_id=1, replica_groups=mesh['dp'=32,'head'=4,'rep'=2] {'rep'}, dimensions={0} | all-to-all | bytes 3538944 | tf_op jit(solution)/shard_map/all_to_all | solution.py:75
  214.7 1.2 copy.38
  (30 shorter events, 1.5 us)
Async XLA Ops:
  10.3 26.9 %all-to-all-start.1 = ((bf16[128,2,8]{2,1,0:T(2,128)(2,1)}), bf16[128,2,8]{2,1,0:T(2,128)(2,1)S(1)}, u32[]{:S(2)}, u32[]{:S(2)}) async-start(bf16[128,2,8]{2,1,0:T(2,128)(2,1)} %bitcast.4), calls=%async_computation.1 | async-start | bytes 131072 | tf_op jit(solution)/shard_map/all_to_all | solution.py:43
  37.2 10.5 %copy-start.4 = (bf16[1,768]{1,0:T(2,128)(2,1)S(1)}, bf16[1,768]{1,0:T(2,128)(2,1)}, u32[]{:S(2)}) copy-start(bf16[1,768]{1,0:T(2,128)(2,1)} %param.15) | copy-start | bytes 4612
  37.2 10.5 %copy-start.5 = (bf16[1,768]{1,0:T(2,128)(2,1)S(1)}, bf16[1,768]{1,0:T(2,128)(2,1)}, u32[]{:S(2)}) copy-start(bf16[1,768]{1,0:T(2,128)(2,1)} %param.14) | copy-start | bytes 4612
  37.2 114.4 %copy-start.3 = (bf16[1,1152,768]{2,1,0:T(8,128)(2,1)S(1)}, bf16[1,1152,768]{2,1,0:T(8,128)(2,1)}, u32[]{:S(2)}) copy-start(bf16[1,1152,768]{2,1,0:T(8,128)(2,1)} %param.13) | copy-start | bytes 5308420
  37.2 114.4 %all-to-all-start = ((bf16[128,2,8,1152]{3,2,1,0:T(8,128)(2,1)}), bf16[128,2,8,1152]{3,2,1,0:T(8,128)(2,1)}, u32[]{:S(2)}, u32[]{:S(2)}) async-start(bf16[128,2,8,1152]{3,2,1,0:T(8,128)(2,1)} %bitcast.59), calls=%async_computation | async-start | bytes 9437184 | tf_op jit(solution)/shard_map/all_to_all | solution.py:42
  47.5 157.4 %all-reduce.2.cloned.1.call-start = ((), (), s32[]{:S(2)}) async-start(), calls=%async_computation.3 | async-start | bytes 7077888 | tf_op jit(solution)/shard_map/psum | solution.py:66
  158.5 2.7 %copy-start = (f32[2048,768]{1,0:T(8,128)}, f32[2048,768]{1,0:T(8,128)S(1)}, u32[]{:S(2)}) copy-start(f32[2048,768]{1,0:T(8,128)S(1)} %get-tuple-element.15) | copy-start | bytes 18874372
  170.3 34.6 %copy-start.1 = (f32[1,576,768]{2,1,0:T(8,128)S(1)}, f32[1,576,768]{2,1,0:T(8,128)}, u32[]{:S(2)}) copy-start(f32[1,576,768]{2,1,0:T(8,128)} %param.17) | copy-start | bytes 5308420
  170.3 34.6 %copy-start.2 = (f32[1,576,768]{2,1,0:T(8,128)S(1)}, f32[1,576,768]{2,1,0:T(8,128)}, u32[]{:S(2)}) copy-start(f32[1,576,768]{2,1,0:T(8,128)} %param.16) | copy-start | bytes 5308420
Sparse Core Ops, SparseCore 0:
  170.4 34.4 all-reduce.1
